TPU v7x, 512 devices: a whole 4x4x16 slice. The times are simulated.
512 devices in a mesh: dp: 8 (over x_hi, y), fsdp: 64 (over z, x_lo, core).
Axes of the slice: x: 4 (x_hi: 2, x_lo: 2; x = x_hi * 2 + x_lo), y: 4, z: 16, core: 2. Of those that a mesh axis runs over, the one named last changes fastest.
Arguments:
- samples: bfloat16 [1024, 256, 768], P(('dp', 'fsdp')), may hold values from -6 to 6
- cotangent: bfloat16 [1024, 256, 768], P(('dp', 'fsdp')), may hold values from -6 to 6
- w_in: bfloat16 [3072, 768], P('fsdp'), may hold values from -0.21875 to 0.21875
- w_out: bfloat16 [3072, 768], P('fsdp'), may hold values from -0.21875 to 0.21875
- sketch_in: bfloat16 [768, 16], replicated, may hold values from -0.21875 to 0.21875
- sketch_hidden: bfloat16 [3072, 16], replicated, may hold values from -0.109375 to 0.109375
- targets: float32 [1024], P(('dp', 'fsdp')), may hold values from -6 to 6
Outputs:
- coeffs: float32 [1024], P(('dp', 'fsdp'))
- sketched_step: float32 [512], replicated
All inputs are finite; a program needn't handle non-finite values.
Results may differ from a plain program's by a relative error of at most 0.0054.
Values may be sent and summed in bfloat16 or wider, within the bound.
A program may use at most 64 MiB of HBM per device.

v0:
```python
import jax
import jax.numpy as jnp
from jax import lax
from jax.sharding import PartitionSpec as P

DAMPING = 0.5


def per_device(samples, cotangent, w_in, w_out, sketch_in, sketch_hidden, targets):
    count, length, width = samples.shape
    flat_x = samples.reshape(count * length, width)
    flat_g = cotangent.reshape(count * length, width)
    rows_in = lax.all_gather(w_in, "fsdp", axis=0, tiled=True)
    rows_out = lax.all_gather(w_out, "fsdp", axis=0, tiled=True)
    all_targets = lax.all_gather(targets, ("dp", "fsdp"), axis=0, tiled=True)
    pre = lax.dot_general(
        flat_x, rows_in, (((1,), (1,)), ((), ())), preferred_element_type=jnp.float32
    )
    back = lax.dot_general(
        flat_g, rows_out, (((1,), (1,)), ((), ())), preferred_element_type=jnp.float32
    )
    sig = jax.nn.sigmoid(pre)
    hidden = (pre * sig).astype(jnp.bfloat16)
    slope = (back * sig * (1.0 + pre * (1.0 - sig))).astype(jnp.bfloat16)
    hq = jnp.dot(hidden, sketch_hidden, preferred_element_type=jnp.float32)
    dq = jnp.dot(slope, sketch_hidden, preferred_element_type=jnp.float32)
    xp = jnp.dot(flat_x, sketch_in, preferred_element_type=jnp.float32)
    gp = jnp.dot(flat_g, sketch_in, preferred_element_type=jnp.float32)

    def outer(left, right):
        return (
            jnp.einsum(
                "spr,spq->srq",
                left.reshape(count, length, -1),
                right.reshape(count, length, -1),
                precision=lax.Precision.HIGHEST,
            )
            / length
        ).reshape(count, -1)

    feats = jnp.concatenate([outer(dq, xp), outer(hq, gp)], axis=1).astype(jnp.bfloat16)
    everyone = lax.all_gather(feats, ("dp", "fsdp"), axis=0, tiled=True)
    size = feats.shape[1]
    small = lax.dot_general(
        everyone, everyone, (((0,), (0,)), ((), ())), preferred_element_type=jnp.float32
    )
    right = lax.dot_general(
        everyone.astype(jnp.float32),
        all_targets,
        (((0,), (0,)), ((), ())),
        precision=lax.Precision.HIGHEST,
    )
    factor = jnp.linalg.cholesky(small + DAMPING * jnp.eye(size, dtype=jnp.float32))
    step = jax.scipy.linalg.cho_solve((factor, True), right)
    fitted = jnp.dot(feats.astype(jnp.float32), step, precision=lax.Precision.HIGHEST)
    coeffs = (targets - fitted) / DAMPING
    return (coeffs, step)


def solution(mesh):
    in_specs = (
        P(("dp", "fsdp"), None, None),
        P(("dp", "fsdp"), None, None),
        P("fsdp", None),
        P("fsdp", None),
        P(),
        P(),
        P(("dp", "fsdp")),
    )
    out_specs = (P(("dp", "fsdp")), P())
    return jax.shard_map(
        per_device, mesh=mesh, in_specs=in_specs, out_specs=out_specs, check_vma=False
    )
```

profile of v0, /device:TPU:1, one launch (start us, length us, event | category | flops | bytes accessed | tf_op | source)
XLA Modules:
  0.0 1186.7 jit_solution(7681346825893043996)
XLA Ops:
  9.8 1.5 fusion.44
  11.2 129.1 %all-gather.7.cloned.1.call-done = bf16[3072,768]{1,0:T(8,128)(2,1)} async-done(((bf16[48,768]{1,0:T(8,128)(2,1)}), bf16[3072,768]{1,0:T(8,128)(2,1)}) %all-gather.7.cloned.1.call-update) | async-done | bytes 4718608 | tf_op jit(solution)/shard_map/all_gather | solution.py:13
  140.3 4.6 fusion.74
  144.9 2.6 copy-done.9
  147.5 1.9 fusion
  149.4 113.7 %all-gather.5.cloned.1.call-done = bf16[3072,768]{1,0:T(8,128)(2,1)} async-done(((bf16[48,768]{1,0:T(8,128)(2,1)}), bf16[3072,768]{1,0:T(8,128)(2,1)}) %all-gather.5.cloned.1.call-update) | async-done | bytes 4718608 | tf_op jit(solution)/shard_map/all_gather | solution.py:14
  263.1 8.1 fusion.1
  272.6 102.0 %all-reduce.1 = f32[1024]{0:T(1024)S(1)} all-reduce(f32[1024]{0:T(1024)S(1)} %dynamic-update-slice.23), channel_id=1, replica_groups=mesh['dp'=8,'fsdp'=64] {'dp','fsdp'}, use_global_device_ids=true, to_apply=%add.1 | all-reduce | flops 1024 | bytes 8192
  374.6 661.0 %all-gather.9.cloned.1.call-done = bf16[512,2,512]{2,1,0:T(2,128)(2,1)} async-done(((bf16[1,2,512]{2,1,0:T(2,128)(2,1)}), bf16[512,2,512]{2,1,0:T(2,128)(2,1)}) %all-gather.9.cloned.1.call-update) | async-done | bytes 1048592 | tf_op jit(solution)/shard_map/all_gather | solution.py:42
  1035.7 1.6 reshape.169
  1040.7 11.7 cholesky.103
  1052.5 9.8 custom-call.34
  1064.9 11.7 cholesky.215
  1076.6 10.0 custom-call.35
  1088.2 11.7 cholesky.236
  1100.6 9.8 custom-call.36
  1111.9 11.9 %cholesky.253 = f32[128,128]{1,0:T(8,128)S(1)} custom-call(f32[128,128]{1,0:T(8,128)S(1)} %convolution_subtract_fusion.2), custom_call_target="Cholesky" | custom-call | tf_op jit(solution)/shard_map/jit(cholesky)/cholesky | solution.py:53
  1127.7 7.7 while.1
  1128.4 1.3 bitcast_dynamic-update-slice_fusion.2
  1130.3 1.3 bitcast_dynamic-update-slice_fusion.2
  1132.2 1.3 bitcast_dynamic-update-slice_fusion.2
  1134.1 1.3 bitcast_dynamic-update-slice_fusion.2
  1135.4 39.3 %custom-call.37 = f32[4,128,128]{1,2,0:T(8,128)S(1)} custom-call(f32[4,128,128]{2,1,0:T(8,128)S(1)} %get-tuple-element.9), custom_call_target="InvertDiagBlocksLowerTriangular" | custom-call | tf_op jit(solution)/shard_map/jit(_cho_solve)/triangular_solve | solution.py:54
  1174.7 1.7 fusion.76
  (82 shorter events, 21.2 us)
Async XLA Ops:
  7.2 1.5 copy-start
  7.2 133.1 %all-gather.7.cloned.1.call-start = ((), (), s32[]{:S(2)}) async-start(), calls=%async_computation.1 | async-start | bytes 4792320 | tf_op jit(solution)/shard_map/all_gather | solution.py:13
  7.9 255.2 %all-gather.5.cloned.1.call-start = ((), (), s32[]{:S(2)}) async-start(), calls=%async_computation | async-start | bytes 4792320 | tf_op jit(solution)/shard_map/all_gather | solution.py:14
  8.7 1027.0 %all-gather.9.cloned.1.call-start = ((), (), s32[]{:S(2)}) async-start(), calls=%async_computation.2 | async-start | bytes 1050624 | tf_op jit(solution)/shard_map/all_gather | solution.py:42
  140.3 7.2 copy-start.7
  144.8 2.7 copy-start.9
  147.5 115.6 %copy-start.3 = (bf16[2,256,768]{2,1,0:T(8,128)(2,1)S(1)}, bf16[2,256,768]{2,1,0:T(8,128)(2,1)}, u32[]{:S(2)}) copy-start(bf16[2,256,768]{2,1,0:T(8,128)(2,1)} %param.8) | copy-start | bytes 2359300
  263.1 9.3 copy-start.8
  271.7 0.6 copy-start.4
  1037.3 1.0 copy-start.1
  1039.4 140.1 %copy-start.5 = (bf16[2,512]{1,0:T(2,128)(2,1)S(1)}, bf16[2,512]{1,0:T(2,128)(2,1)}, u32[]{:S(2)}) copy-start(bf16[2,512]{1,0:T(2,128)(2,1)} %copy-done.4) | copy-start | bytes 6148
  1039.6 1.0 copy-start.2
  1179.5 0.7 copy-start.6
Sparse Core Ops, SparseCore 0:
  10.1 130.0 all-gather.6
  142.4 120.6 all-gather.4
  272.4 763.1 all-gather.8
where the time goes:
time: 1190 us
  waiting for transfers between devices  905 us (76%)
  other arithmetic  118 us (10%)
  blocking collectives  102 us (9%)
  matrix products  28.8 us (2%)
  between operations  16.5 us (1%)
  local copies, waits for them, and re-layouts  15.5 us (1%)
    all_gather x1, waiting for transfers between devices, per_device(): everyone = lax.all_gather(feats, ('dp', 'fsdp'), axis=0, tiled=True)  661 us
    all_gather x1, waiting for transfers between devices, per_device(): rows_in = lax.all_gather(w_in, 'fsdp', axis=0, tiled=True)  129 us
    all_gather x1, waiting for transfers between devices, per_device(): rows_out = lax.all_gather(w_out, 'fsdp', axis=0, tiled=True)  114 us
    unnamed x1, blocking collectives  102 us
    another operation x14, other arithmetic, per_device(): jnp.linalg.cholesky(small + DAMPING * jnp.eye(size, dtype=jnp.float32))  78.8 us
    another operation x4, other arithmetic, per_device(): step = jax.scipy.linalg.cho_solve((factor, True), right)  39.5 us
  transfers between devices with their start and end apart: 3, of which 3 were waited for; matrix products, arithmetic and copies ran while one was open for 1% of the time, Pallas kernels for 0%

commit v1 on v0

--- a/solution.py
+++ b/solution.py
@@ -39,7 +39,8 @@
         ).reshape(count, -1)
 
     feats = jnp.concatenate([outer(dq, xp), outer(hq, gp)], axis=1).astype(jnp.bfloat16)
-    everyone = lax.all_gather(feats, ("dp", "fsdp"), axis=0, tiled=True)
+    sent = jnp.stack([feats] * lax.axis_size(("dp", "fsdp")))
+    everyone = jnp.concatenate(lax.all_to_all(sent, ("dp", "fsdp"), 0, 0), axis=0)
     size = feats.shape[1]
     small = lax.dot_general(
         everyone, everyone, (((0,), (0,)), ((), ())), preferred_element_type=jnp.float32

time: 1190 us -> 566 us (0.48)
  waiting for transfers between devices: 905 us -> 244 us
  blocking collectives: 102 us -> 119 us
  starting transfers between devices: 0.11 us -> 14.9 us
    all_gather x1 -> x0, waiting for transfers between devices: 661 us -> none  [per_device(): everyone = lax.all_gather(feats, ('dp', 'fsdp'), axis=0, tiled=True)]
    unnamed x1, blocking collectives: 102 us -> 119 us
    all_to_all x0 -> x1, starting transfers between devices: none -> 14.8 us  [per_device(): lax.all_to_all(sent, ('dp', 'fsdp'), 0, 0)]
  transfers between devices with their start and end apart: 3 -> 3, of which waited for: 3 -> 2; matrix products, arithmetic and copies ran while one was open for 1% -> 2% of each run, Pallas kernels for 0% -> 0%
where the time goes in v1:
time: 566 us; the launch traced here: 558 us
  waiting for transfers between devices  244 us (43%)
  blocking collectives  119 us (21%)
  other arithmetic  118 us (21%)
  matrix products  27.6 us (5%)
  local copies, waits for them, and re-layouts  17.1 us (3%)
  between operations  17.1 us (3%)
  starting transfers between devices  14.9 us (3%)
    all_gather x1, waiting for transfers between devices, per_device(): rows_in = lax.all_gather(w_in, 'fsdp', axis=0, tiled=True)  129 us
    unnamed x1, blocking collectives  119 us
    all_gather x1, waiting for transfers between devices, per_device(): rows_out = lax.all_gather(w_out, 'fsdp', axis=0, tiled=True)  114 us
    another operation x14, other arithmetic, per_device(): jnp.linalg.cholesky(small + DAMPING * jnp.eye(size, dtype=jnp.float32))  78.8 us
    another operation x4, other arithmetic, per_device(): step = jax.scipy.linalg.cho_solve((factor, True), right)  39.5 us
    all_to_all x1, starting transfers between devices, per_device(): lax.all_to_all(sent, ('dp', 'fsdp'), 0, 0)  14.8 us
  transfers between devices with their start and end apart: 3, of which 2 were waited for; matrix products, arithmetic and copies ran while one was open for 2% of the time, Pallas kernels for 0%

profile of v1, /device:TPU:1, one launch (start us, length us, event | category | flops | bytes accessed | tf_op | source)
XLA Modules:
  0.0 558.1 jit_solution(4656263926337969756)
XLA Ops:
  9.7 1.5 fusion.45
  11.2 129.1 %all-gather.5.cloned.1.call-done = bf16[3072,768]{1,0:T(8,128)(2,1)} async-done(((bf16[48,768]{1,0:T(8,128)(2,1)}), bf16[3072,768]{1,0:T(8,128)(2,1)}) %all-gather.5.cloned.1.call-update) | async-done | bytes 4718608 | tf_op jit(solution)/shard_map/all_gather | solution.py:13
  140.3 4.6 fusion.75
  144.9 2.7 copy-done.7
  147.5 1.9 fusion
  149.4 113.7 %all-gather.3.cloned.1.call-done = bf16[3072,768]{1,0:T(8,128)(2,1)} async-done(((bf16[48,768]{1,0:T(8,128)(2,1)}), bf16[3072,768]{1,0:T(8,128)(2,1)}) %all-gather.3.cloned.1.call-update) | async-done | bytes 4718608 | tf_op jit(solution)/shard_map/all_gather | solution.py:14
  263.1 8.1 %fusion.1 = f32[512,16]{0,1:T(8,128)S(1)} fusion(bf16[3072,16]{0,1:T(8,128)(2,1)S(1)} %copy-done.5, f32[512,3072]{1,0:T(8,128)} %copy-done.7, bf16[512,768]{1,0:T(8,128)(2,1)S(1)} %bitcast.180, bf16[3072,768]{1,0:T(8,128)(2,1)} %all-gather.3.cloned.1.call-done), kind=kOutput, calls=%fused_computation.6 | convolution fusion | flops 2480406528 | bytes 11927552 | tf_op jit(solution)/shard_map/dot_general | solution.py:26
  271.7 1.5 stack.2
  273.3 14.8 %all-to-all-start = ((bf16[512,2,512]{2,1,0:T(2,128)(2,1)}), bf16[512,2,512]{2,1,0:T(2,128)(2,1)S(1)}, u32[]{:S(2)}, u32[]{:S(2)}) async-start(bf16[512,2,512]{2,1,0:T(2,128)(2,1)} %stack.2), calls=%async_computation | async-start | bytes 2097152 | tf_op jit(solution)/shard_map/all_to_all | solution.py:43
  288.4 118.7 %all-reduce.1 = f32[1024]{0:T(1024)S(1)} all-reduce(f32[1024]{0:T(1024)S(1)} %dynamic-update-slice.23), channel_id=1, replica_groups=mesh['dp'=8,'fsdp'=64] {'dp','fsdp'}, use_global_device_ids=true, to_apply=%add.1 | all-reduce | flops 1024 | bytes 8192
  410.5 11.7 %cholesky.103 = f32[128,128]{1,0:T(8,128)S(1)} custom-call(f32[128,128]{1,0:T(8,128)S(1)} %cholesky.263), custom_call_target="Cholesky" | custom-call | tf_op jit(solution)/shard_map/jit(cholesky)/cholesky | solution.py:54
  422.3 9.8 %custom-call.34 = f32[1,128,128]{1,2,0:T(8,128)S(1)} custom-call(f32[1,128,128]{2,1,0:T(8,128)S(1)} %get-tuple-element.29), custom_call_target="InvertDiagBlocksLowerTriangular" | custom-call | tf_op jit(solution)/shard_map/jit(cholesky)/cholesky | solution.py:54
  434.7 11.7 %cholesky.215 = f32[128,128]{1,0:T(8,128)S(1)} custom-call(f32[128,128]{1,0:T(8,128)S(1)} %cholesky.267), custom_call_target="Cholesky" | custom-call | tf_op jit(solution)/shard_map/jit(cholesky)/cholesky | solution.py:54
  446.4 10.0 %custom-call.35 = f32[1,128,128]{1,2,0:T(8,128)S(1)} custom-call(f32[1,128,128]{2,1,0:T(8,128)S(1)} %get-tuple-element.26), custom_call_target="InvertDiagBlocksLowerTriangular" | custom-call | tf_op jit(solution)/shard_map/jit(cholesky)/cholesky | solution.py:54
  458.0 11.7 %cholesky.236 = f32[128,128]{1,0:T(8,128)S(1)} custom-call(f32[128,128]{1,0:T(8,128)S(1)} %cholesky.272), custom_call_target="Cholesky" | custom-call | tf_op jit(solution)/shard_map/jit(cholesky)/cholesky | solution.py:54
  470.4 9.8 %custom-call.36 = f32[1,128,128]{1,2,0:T(8,128)S(1)} custom-call(f32[1,128,128]{2,1,0:T(8,128)S(1)} %get-tuple-element.23), custom_call_target="InvertDiagBlocksLowerTriangular" | custom-call | tf_op jit(solution)/shard_map/jit(cholesky)/cholesky | solution.py:54
  481.6 11.9 %cholesky.253 = f32[128,128]{1,0:T(8,128)S(1)} custom-call(f32[128,128]{1,0:T(8,128)S(1)} %convolution_subtract_fusion.2), custom_call_target="Cholesky" | custom-call | tf_op jit(solution)/shard_map/jit(cholesky)/cholesky | solution.py:54
  497.6 8.5 %while.1 = (s32[]{:T(128)}, f32[512,512]{1,0:T(8,128)S(1)}, s32[4,2]{0,1:T(2,128)S(1)}, f32[4,128,128]{2,1,0:T(8,128)S(1)}, s32[]{:T(128)}) while((s32[]{:T(128)}, f32[512,512]{1,0:T(8,128)S(1)}, s32[4,2]{0,1:T(2,128)S(1)}, f32[4,128,128]{2,1,0:T(8,128)S(1)}, s32[]{:T(128)}) %tuple.31), condition=%wide.while_cond, body=%wide.while_body.sunk | while | flops 2 | bytes 131181 | solution.py:55
  498.3 1.4 bitcast_dynamic-update-slice_fusion.2
  500.4 1.4 bitcast_dynamic-update-slice_fusion.2
  502.5 1.4 bitcast_dynamic-update-slice_fusion.2
  504.6 1.4 bitcast_dynamic-update-slice_fusion.2
  506.1 39.3 %custom-call.37 = f32[4,128,128]{1,2,0:T(8,128)S(1)} custom-call(f32[4,128,128]{2,1,0:T(8,128)S(1)} %get-tuple-element.9), custom_call_target="InvertDiagBlocksLowerTriangular" | custom-call | tf_op jit(solution)/shard_map/jit(_cho_solve)/triangular_solve | solution.py:55
  545.4 1.5 reshape.155
  (78 shorter events, 21.3 us)
Async XLA Ops:
  7.2 1.5 copy-start
  7.2 133.1 %all-gather.5.cloned.1.call-start = ((), (), s32[]{:S(2)}) async-start(), calls=%async_computation.2 | async-start | bytes 4792320 | tf_op jit(solution)/shard_map/all_gather | solution.py:13
  7.9 255.2 %all-gather.3.cloned.1.call-start = ((), (), s32[]{:S(2)}) async-start(), calls=%async_computation.1 | async-start | bytes 4792320 | tf_op jit(solution)/shard_map/all_gather | solution.py:14
  140.3 7.2 %copy-start.5 = (bf16[3072,16]{0,1:T(8,128)(2,1)S(1)}, bf16[3072,16]{0,1:T(8,128)(2,1)}, u32[]{:S(2)}) copy-start(bf16[3072,16]{0,1:T(8,128)(2,1)} %param.12) | copy-start | bytes 294916
  144.8 2.7 copy-start.7
  147.5 115.6 %copy-start.3 = (bf16[2,256,768]{2,1,0:T(8,128)(2,1)S(1)}, bf16[2,256,768]{2,1,0:T(8,128)(2,1)}, u32[]{:S(2)}) copy-start(bf16[2,256,768]{2,1,0:T(8,128)(2,1)} %param.8) | copy-start | bytes 2359300
  263.1 25.0 %copy-start.6 = (f32[2]{0:T(128)S(1)}, f32[2]{0:T(128)}, u32[]{:S(2)}) copy-start(f32[2]{0:T(128)} %param.13) | copy-start | bytes 28
  273.3 133.8 %all-to-all-start = ((bf16[512,2,512]{2,1,0:T(2,128)(2,1)}), bf16[512,2,512]{2,1,0:T(2,128)(2,1)S(1)}, u32[]{:S(2)}, u32[]{:S(2)}) async-start(bf16[512,2,512]{2,1,0:T(2,128)(2,1)} %stack.2), calls=%async_computation | async-start | bytes 2097152 | tf_op jit(solution)/shard_map/all_to_all | solution.py:43
  407.1 1.0 copy-start.1
  409.4 1.0 copy-start.2
  550.3 0.7 copy-start.4
Sparse Core Ops, SparseCore 0:
  10.1 130.0 all-gather.4
  142.4 120.6 all-gather.2
